TPU v7x, 128 devices: a whole 4x4x4 slice. The times are simulated.
128 devices in a mesh: row: 8 (over z, core), col: 16 (over x, y).
Axes of the slice: x: 4, y: 4, z: 4, core: 2. Of those that a mesh axis runs over, the one named last changes fastest.
Arguments:
- tile_values: float32 [2048, 512, 512], P(('row', 'col')), may hold values from -6 to 6
- tile_coords: int32 [2048, 2], P(('row', 'col')), may hold values from 0 to 3, as said below
- tile_counts: int32 [128], P(('row', 'col')), may hold values from 4 to 16, as said below
- restrict_basis: float32 [16384, 256], P(('row', 'col')), may hold values from -0.25 to 0.25
- prolong_basis: float32 [32768, 256], P(('col', 'row')), may hold values from -0.25 to 0.25
- row_partner: int32 [16, 8], replicated, may hold values from 0 to 7, as said below
- col_partner: int32 [8, 16], replicated, may hold values from 0 to 15, as said below
Outputs:
- coarse: float32 [4096, 8192], P('row', 'col')
Inputs may be any that keep to these rules, and one draw needn't show every extreme that they name: `tile_coords`: within one device's 16 slots no two name the same (block row, block column); first entry below 4, second below 4; dead slots also hold such positions. `tile_counts`: number of leading slots of each device that are live; some device has all 16 live. `row_partner`: each row is a pairing: the partner of a part's partner is the part itself, never the part. `col_partner`: each row is a pairing: the partner of a part's partner is the part itself, never the part.
All inputs are finite; a program needn't handle non-finite values.
Results may differ from a plain program's by a relative error of at most 0.0003.
Values sent between devices are 32-bit elements; how exact they have to be, the bound alone decides.
A program may use at most 128 MiB of HBM per device.

v0:
```python
import jax
import jax.numpy as jnp
from jax import lax
from jax.sharding import PartitionSpec as P


def pick_half(block, keep_flag, axis_dim):
    half_size = block.shape[axis_dim] // 2
    first = lax.slice_in_dim(block, 0, half_size, 1, axis_dim)
    second = lax.slice_in_dim(block, half_size, 2 * half_size, 1, axis_dim)
    kept = jnp.where(keep_flag, second, first)
    given = jnp.where(keep_flag, first, second)
    return (kept, given)


def body(
    tile_values, tile_coords, tile_counts, restrict_basis, prolong_basis, row_partner, col_partner
):
    restrict_part = lax.all_gather(restrict_basis, "col", axis=0, tiled=True)
    prolong_part = lax.all_gather(prolong_basis, "row", axis=0, tiled=True)
    tile_order = tile_values.shape[1]
    basis_width = restrict_basis.shape[1]
    block_rows = restrict_part.shape[0] // tile_order
    block_cols = prolong_part.shape[0] // tile_order
    live_count = tile_counts[0]

    def add_slot(slot_index, grid_now):
        block_row = tile_coords[slot_index, 0]
        block_col = tile_coords[slot_index, 1]
        left = lax.dynamic_slice_in_dim(restrict_part, block_row * tile_order, tile_order, 0)
        right = lax.dynamic_slice_in_dim(prolong_part, block_col * tile_order, tile_order, 0)
        applied = jnp.dot(tile_values[slot_index], right, precision=lax.Precision.HIGHEST)
        product = jnp.dot(left.T, applied, precision=lax.Precision.HIGHEST)
        product = jnp.where(slot_index < live_count, product, jnp.zeros_like(product))
        place = (block_row * basis_width, block_col * basis_width)
        current = lax.dynamic_slice(grid_now, place, (basis_width, basis_width))
        return lax.dynamic_update_slice(grid_now, current + product, place)

    start_grid = jnp.zeros((block_rows * basis_width, block_cols * basis_width), jnp.float32)
    local_grid = lax.fori_loop(0, tile_values.shape[0], add_slot, start_grid)
    my_row = lax.axis_index("row")
    my_col = lax.axis_index("col")
    row_table = row_partner[my_col]
    col_table = col_partner[my_row]
    partner_row = row_table[my_row]
    partner_col = col_table[my_col]
    keep_row = my_row > partner_row
    keep_col = my_col > partner_col
    kept, given = pick_half(local_grid, keep_row, 0)
    height = kept.shape[0]
    gathered = lax.all_gather(given, "row", axis=0, tiled=True)
    incoming = lax.dynamic_slice_in_dim(gathered, partner_row * height, height, 0)
    row_section = kept + incoming
    kept, given = pick_half(row_section, keep_col, 1)
    breadth = kept.shape[1]
    gathered = lax.all_gather(given, "col", axis=1, tiled=True)
    incoming = lax.dynamic_slice_in_dim(gathered, partner_col * breadth, breadth, 1)
    return kept + incoming


def solution(mesh):
    in_specs = (
        P(("row", "col"), None, None),
        P(("row", "col"), None),
        P(("row", "col")),
        P(("row", "col"), None),
        P(("col", "row"), None),
        P(),
        P(),
    )
    out_specs = P("row", "col")
    return jax.shard_map(body, mesh=mesh, in_specs=in_specs, out_specs=out_specs, check_vma=False)
```

profile of v0, /device:TPU:1, one launch (start us, length us, event | category | flops | bytes accessed | tf_op | source)
XLA Modules:
  0.0 450.1 jit_solution(11749270185741397715)
XLA Ops:
  6.5 0.7 all-gather.7.cloned.1.call-update
  7.3 0.7 all-gather.5.cloned.1.call-update
  8.1 1.3 dynamic_slice.57
  10.1 28.1 %all-gather.7.cloned.1.call-done = f32[2048,256]{1,0:T(8,128)} async-done(((f32[256,256]{1,0:T(8,128)}), f32[2048,256]{1,0:T(8,128)}) %all-gather.7.cloned.1.call-update) | async-done | bytes 2097168 | tf_op jit(solution)/shard_map/all_gather | solution.py:20
  38.2 45.2 %all-gather.5.cloned.1.call-done = f32[2048,256]{1,0:T(8,128)} async-done(((f32[128,256]{1,0:T(8,128)}), f32[2048,256]{1,0:T(8,128)}) %all-gather.5.cloned.1.call-update) | async-done | bytes 2097168 | tf_op jit(solution)/shard_map/all_gather | solution.py:19
  83.4 2.5 broadcast_in_dim.3
  85.9 148.6 %while.13 = (s32[]{:T(128)}, f32[1024,1024]{1,0:T(8,128)}, s32[16,2]{0,1:T(2,128)S(1)}, s32[]{:T(128)}, f32[2048,256]{1,0:T(8,128)}, /*index=5*/f32[16,512,512]{...) while((s32[]{:T(128)}, f32[1024,1024]{1,0:T(8,128)}, ...), condition=%wide.region_1.2_spmd, body=%wide.region_0.1_spmd.sunk | while | flops 1208090624 | bytes 3670383 | solution.py:40
  89.9 2.3 fusion.20
  92.3 2.9 fusion.21
  99.2 2.3 fusion.20
  101.6 2.8 fusion.21
  108.5 2.3 fusion.20
  110.8 2.9 fusion.21
  117.8 2.3 fusion.20
  120.1 2.9 fusion.21
  127.1 2.3 fusion.20
  129.4 2.9 fusion.21
  136.4 2.3 fusion.20
  138.7 2.9 fusion.21
  142.3 0.7 constant_dynamic-slice_fusion.3
  145.7 2.3 fusion.20
  148.0 2.9 fusion.21
  154.9 2.3 fusion.20
  157.3 2.9 fusion.21
  164.2 2.3 fusion.20
  166.6 2.9 fusion.21
  173.5 2.3 fusion.20
  175.8 2.9 fusion.21
  182.8 2.3 fusion.20
  185.2 2.9 fusion.21
  188.7 0.7 constant_dynamic-slice_fusion.3
  192.1 2.3 fusion.20
  194.5 2.8 fusion.21
  201.4 2.3 fusion.20
  203.7 2.9 fusion.21
  210.6 2.3 fusion.20
  213.0 2.9 fusion.21
  219.9 2.4 fusion.20
  222.3 2.9 fusion.21
  229.2 2.3 fusion.20
  231.5 2.9 fusion.21
  234.4 4.1 slice_select_fusion
  238.6 1.3 dynamic_slice.56
  241.3 83.9 %all-gather.9.cloned.1.call-done = f32[4096,1024]{1,0:T(8,128)} async-done(((f32[512,1024]{1,0:T(8,128)}), f32[4096,1024]{1,0:T(8,128)}) %all-gather.9.cloned.1.call-update) | async-done | bytes 16777232 | tf_op jit(solution)/shard_map/all_gather | solution.py:51
  325.2 3.5 dynamic-slice_add_fusion
  328.7 1.2 slice_select_fusion.1
  330.6 110.5 %all-gather.11.cloned.1.call-done = f32[512,8192]{1,0:T(8,128)} async-done(((f32[512,512]{1,0:T(8,128)}), f32[512,8192]{1,0:T(8,128)}) %all-gather.11.cloned.1.call-update) | async-done | bytes 16777232 | tf_op jit(solution)/shard_map/all_gather | solution.py:56
  441.0 2.5 dynamic-slice_add_fusion.1
  (22 shorter events, 9.5 us)
Async XLA Ops:
  6.5 31.7 %all-gather.7.cloned.1.call-start = ((), (), s32[]{:S(2)}) async-start(), calls=%async_computation.1 | async-start | bytes 2359296 | tf_op jit(solution)/shard_map/all_gather | solution.py:20
  7.3 76.1 %all-gather.5.cloned.1.call-start = ((), (), s32[]{:S(2)}) async-start(), calls=%async_computation | async-start | bytes 2228224 | tf_op jit(solution)/shard_map/all_gather | solution.py:19
  8.0 317.2 %all-gather.9.cloned.1.call-start = ((), (), s32[]{:S(2)}) async-start(), calls=%async_computation.2 | async-start | bytes 18874368 | tf_op jit(solution)/shard_map/all_gather | solution.py:51
  83.4 2.5 copy-start
  238.6 202.4 %all-gather.11.cloned.1.call-start = ((), (), s32[]{:S(2)}) async-start(), calls=%async_computation.3 | async-start | bytes 17825792 | tf_op jit(solution)/shard_map/all_gather | solution.py:56
Sparse Core Ops, SparseCore 0:
  9.0 29.1 all-gather.6
  40.3 43.0 all-gather.4
  238.7 86.4 all-gather.8
  330.1 110.9 all-gather.10
where the time goes:
time: 452 us; the launch traced here: 450 us
  waiting for transfers between devices  269 us (60%)
  matrix products  83.4 us (18%)
  loops' own time  54.4 us (12%)
  local copies, waits for them, and re-layouts  15.9 us (4%)
  between operations  15.8 us (3%)
  other arithmetic  11.4 us (3%)
    all_gather x1, waiting for transfers between devices, body(): gathered = lax.all_gather(given, 'col', axis=1, tiled=True)  110 us
    all_gather x1, waiting for transfers between devices, body(): gathered = lax.all_gather(given, 'row', axis=0, tiled=True)  83.9 us
    another operation x1, loops' own time, body(): local_grid = lax.fori_loop(0, tile_values.shape[0], add_slot, start_grid)  54.4 us
    dot_general x16, matrix products, add_slot(): product = jnp.dot(left.T, applied, precision=lax.Precision.HIGHEST)  45.9 us
    all_gather x1, waiting for transfers between devices, body(): restrict_part = lax.all_gather(restrict_basis, 'col', axis=0, tiled=True)  45.2 us
    dot_general x16, matrix products, add_slot(): jnp.dot(tile_values[slot_index], right, precision=lax.Precision.HIGHEST)  37.6 us
    all_gather x1, waiting for transfers between devices, body(): prolong_part = lax.all_gather(prolong_basis, 'row', axis=0, tiled=True)  28.1 us
    dynamic_slice x16, local copies, waits for them, and re-layouts, add_slot(): block_col = tile_coords[slot_index, 1]  10.7 us
  transfers between devices with their start and end apart: 4, of which 4 were waited for; matrix products, arithmetic and copies ran while one was open for 1% of the time, Pallas kernels for 0%

commit v1 on v0

v1 whole, which is shorter than its diff:
```python
import jax
import jax.numpy as jnp
from jax import lax
from jax.experimental import pallas as pl
from jax.experimental.pallas import tpu as pltpu
from jax.sharding import PartitionSpec as P

MESH = pl.DeviceIdType.MESH
HIGH = lax.Precision.HIGH

TB = 512
K = 256
RB = 4
CB = 4
SLOTS = 16
N_ROW = 8
N_COL = 16
CH = 4
SL = K // N_ROW

Z_PEERS = ((1, 0), (3, 0), (2, 0), (1, 1), (3, 1), (2, 1), (0, 1))
XY_PEERS = tuple(
    sorted(
        ((dx, dy) for dx in range(4) for dy in range(4) if dx or dy),
        key=lambda d: (min(d[0], 4 - d[0]) + min(d[1], 4 - d[1]), d),
    )
)


def kernel(
    tiles_hbm,
    q_ref,
    p_hbm,
    coords,
    counts,
    row_partner,
    col_partner,
    out_ref,
    tiles,
    pbuf,
    qt,
    ubuf,
    gv,
    kept,
    recv1_0,
    recv1_1,
    recv1_2,
    recv1_3,
    snd2,
    inc,
    cs,
    crecv_0,
    crecv_1,
    csnd2,
    cinc,
    slot_sm,
    live_sm,
    tile_sem,
    own_sem,
    p_send,
    p_fsend,
    p_recv,
    q_send,
    q_recv,
    s1_send,
    s1_recv,
    s2_send,
    s2_recv,
    x1_send,
    x1_recv,
    x2_send,
    x2_recv,
):
    recv1 = (recv1_0, recv1_1, recv1_2, recv1_3)
    crecv = (crecv_0, crecv_1)
    r = lax.axis_index("row")
    c = lax.axis_index("col")
    z, core = r // 2, r % 2
    x, y = c // 4, c % 4

    tile_cp = pltpu.make_async_copy(tiles_hbm, tiles, tile_sem)
    tile_cp.start()
    own_cp = pltpu.make_async_copy(p_hbm, pbuf.at[z, core], own_sem)
    own_cp.start()

    z_peers = [((z + dz) % 4) * 2 + (core + dc) % 2 for dz, dc in Z_PEERS]
    xy_peers = [((x + dx) % 4) * 4 + (y + dy) % 4 for dx, dy in XY_PEERS]

    barrier = pltpu.get_barrier_semaphore()
    for peer in z_peers:
        pl.semaphore_signal(barrier, inc=1, device_id={"row": peer}, device_id_type=MESH)
    for peer in xy_peers:
        pl.semaphore_signal(barrier, inc=1, device_id={"col": peer}, device_id_type=MESH)

    qt[x, y] = q_ref[...].T

    for pos in range(RB * CB):
        slot = jnp.int32(0)
        for s in range(SLOTS):
            hit = coords[s, 0] * CB + coords[s, 1] == pos
            slot = jnp.where(hit, jnp.int32(s), slot)
        slot_sm[pos] = slot
        live_sm[pos] = jnp.where(slot < counts[0], jnp.int32(1), jnp.int32(0))

    pl.semaphore_wait(barrier, len(z_peers) + len(xy_peers))

    sibling = z * 2 + (1 - core)
    p_cps = []
    for n, dz in enumerate((1, 3, 2)):
        cp = pltpu.make_async_remote_copy(
            src_ref=p_hbm,
            dst_ref=pbuf.at[z, core],
            send_sem=p_send.at[n],
            recv_sem=p_recv.at[z, core],
            device_id={"row": ((z + dz) % 4) * 2 + core},
            device_id_type=MESH,
        )
        cp.start()
        p_cps.append(cp)
    cp = pltpu.make_async_remote_copy(
        src_ref=p_hbm,
        dst_ref=pbuf.at[z, core],
        send_sem=p_send.at[3],
        recv_sem=p_recv.at[z, core],
        device_id={"row": sibling},
        device_id_type=MESH,
    )
    cp.start()
    p_cps.append(cp)

    def q_copy(ref, n, recv, dest):
        return pltpu.make_async_remote_copy(
            src_ref=ref,
            dst_ref=ref,
            send_sem=q_send.at[n],
            recv_sem=recv,
            device_id={"col": dest},
            device_id_type=MESH,
        )

    half = K // 2
    q_cps = []
    for n, d in enumerate((1, 3, 2)):
        cp = q_copy(qt.at[x, y, pl.ds(0, half)], n, q_recv.at[0, x], ((x + d) % 4) * 4 + y)
        cp.start()
        q_cps.append(cp)
        cp = q_copy(qt.at[x, y, pl.ds(half, half)], 3 + n, q_recv.at[1, y], x * 4 + (y + d) % 4)
        cp.start()
        q_cps.append(cp)
    for d in (1, 3, 2):
        xs, ys = (x + d) % 4, (y + d) % 4
        q_copy(qt.at[xs, y, pl.ds(0, half)], 0, q_recv.at[0, xs], c).wait_recv()
        q_copy(qt.at[x, ys, pl.ds(half, half)], 0, q_recv.at[1, ys], c).wait_recv()
    for n, d in enumerate((1, 3, 2)):
        cp = q_copy(qt.at[:, y, pl.ds(0, half)], 6 + n, q_recv.at[2, y], x * 4 + (y + d) % 4)
        cp.start()
        q_cps.append(cp)
        cp = q_copy(qt.at[x, :, pl.ds(half, half)], 9 + n, q_recv.at[3, x], ((x + d) % 4) * 4 + y)
        cp.start()
        q_cps.append(cp)

    def p_wait(zs, cs_):
        pltpu.make_async_copy(pbuf.at[zs, cs_], pbuf.at[zs, cs_], p_recv.at[zs, cs_]).wait()

    def p_forward(n, zs):
        cp = pltpu.make_async_remote_copy(
            src_ref=pbuf.at[zs, core],
            dst_ref=pbuf.at[zs, core],
            send_sem=p_fsend.at[n],
            recv_sem=p_recv.at[zs, core],
            device_id={"row": sibling},
            device_id_type=MESH,
        )
        cp.start()
        p_cps.append(cp)

    def apply_block(b):
        def one(a, carry):
            right = pbuf[b].reshape(TB, K)
            pos = a * CB + b
            tile = tiles[slot_sm[pos]]
            ubuf[pos] = jnp.dot(tile, right, precision=HIGH, preferred_element_type=jnp.float32)
            return carry

        lax.fori_loop(0, RB, one, 0)

    own_cp.wait()
    p_wait(z, 1 - core)
    tile_cp.wait()
    apply_block(z)
    for n, d in enumerate((1, 3)):
        zs = (z + d) % 4
        p_wait(zs, core)
        p_forward(n, zs)
    for d in (1, 3):
        zs = (z + d) % 4
        p_wait(zs, 1 - core)
        apply_block(zs)
    zs = (z + 2) % 4
    p_wait(zs, core)
    p_forward(2, zs)
    p_wait(zs, 1 - core)
    apply_block(zs)

    for d in (1, 3, 2):
        xs, ys = (x + d) % 4, (y + d) % 4
        q_copy(qt.at[:, ys, pl.ds(0, half)], 0, q_recv.at[2, ys], c).wait_recv()
        q_copy(qt.at[xs, :, pl.ds(half, half)], 0, q_recv.at[3, xs], c).wait_recv()

    my_rp = row_partner[c, r]
    my_cp = col_partner[r, c]
    my_h = jnp.where(r > my_rp, jnp.int32(1), jnp.int32(0))
    my_g = jnp.where(c > my_cp, jnp.int32(1), jnp.int32(0))
    partner_g = jnp.where(c > col_partner[my_rp, c], jnp.int32(1), jnp.int32(0))

    def blocks(dst, ch, row_half, keep_col):
        a = 2 * row_half + ch % 2
        col_half = (1 - keep_col) if ch < 2 else keep_col

        def one(n, carry):
            pos = a * CB + 2 * col_half + n
            left = jnp.concatenate([qt[a, i] for i in range(4)], axis=1)
            g = jnp.dot(left, ubuf[pos], precision=HIGH, preferred_element_type=jnp.float32)
            g = jnp.where(live_sm[pos] > 0, g, jnp.zeros_like(g))
            dst[ch, :, n] = g.reshape(N_ROW, SL, K)
            return carry

        lax.fori_loop(0, 2, one, 0)

    def send1(ch):
        recv1[ch][r] = gv[ch, r]
        for peer in z_peers:
            pltpu.make_async_remote_copy(
                src_ref=gv.at[ch, peer],
                dst_ref=recv1[ch].at[r],
                send_sem=s1_send.at[ch],
                recv_sem=s1_recv.at[ch],
                device_id={"row": peer},
                device_id_type=MESH,
            ).start()

    def take(ref, n, sem):
        view = ref.at[pl.ds(0, n)]
        pltpu.make_async_copy(view, view, sem).wait()

    def send2(ch):
        take(recv1[ch], N_ROW - 1, s1_recv.at[ch])

        def one(k, carry):
            snd2[ch, k] = recv1[ch][row_partner[c, k]]
            return carry

        lax.fori_loop(0, N_ROW, one, 0)
        inc[ch, r] = snd2[ch, r]
        for peer in z_peers:
            pltpu.make_async_remote_copy(
                src_ref=snd2.at[ch, peer],
                dst_ref=inc.at[ch, r],
                send_sem=s2_send.at[ch],
                recv_sem=s2_recv.at[ch],
                device_id={"row": peer},
                device_id_type=MESH,
            ).start()

    def cross1(ch):
        take(inc.at[ch], N_ROW - 1, s2_recv.at[ch])
        cs[ch] = (kept[ch] + inc[ch]).reshape(N_COL, SL, K)
        crecv[ch][c] = cs[ch, c]
        for peer in xy_peers:
            pltpu.make_async_remote_copy(
                src_ref=cs.at[ch, peer],
                dst_ref=crecv[ch].at[c],
                send_sem=x1_send.at[ch],
                recv_sem=x1_recv.at[ch],
                device_id={"col": peer},
                device_id_type=MESH,
            ).start()

    def cross2(ch):
        take(crecv[ch], N_COL - 1, x1_recv.at[ch])

        def one(k, carry):
            csnd2[ch, k] = crecv[ch][col_partner[r, k]]
            return carry

        lax.fori_loop(0, N_COL, one, 0)
        cinc[ch, c] = csnd2[ch, c]
        for peer in xy_peers:
            pltpu.make_async_remote_copy(
                src_ref=csnd2.at[ch, peer],
                dst_ref=cinc.at[ch, c],
                send_sem=x2_send.at[ch],
                recv_sem=x2_recv.at[ch],
                device_id={"col": peer},
                device_id_type=MESH,
            ).start()

    def finish(a):
        take(inc.at[2 + a], N_ROW - 1, s2_recv.at[2 + a])
        take(cinc.at[a], N_COL - 1, x2_recv.at[a])
        for n in range(2):
            total = kept[2 + a, :, n] + inc[2 + a, :, n]
            total = total + cinc[a].reshape(N_ROW, 2, SL, K)[:, n]
            out_ref[a * K : (a + 1) * K, n * K : (n + 1) * K] = total.reshape(K, K)

    given_h = 1 - my_h
    blocks(gv, 0, given_h, partner_g)
    send1(0)
    blocks(gv, 1, given_h, partner_g)
    send1(1)
    blocks(gv, 2, given_h, partner_g)
    blocks(gv, 3, given_h, partner_g)
    for ch in range(CH):
        blocks(kept, ch, my_h, my_g)
    send2(0)
    send2(1)
    send1(2)
    send1(3)
    cross1(0)
    cross1(1)
    cross2(0)
    send2(2)
    cross2(1)
    send2(3)
    finish(0)
    finish(1)

    for cp in p_cps + q_cps:
        cp.wait_send()
    for ch in range(CH):
        take(gv.at[ch], N_ROW - 1, s1_send.at[ch])
        take(snd2.at[ch], N_ROW - 1, s2_send.at[ch])
    for ch in range(2):
        take(cs.at[ch], N_COL - 1, x1_send.at[ch])
        take(csnd2.at[ch], N_COL - 1, x2_send.at[ch])


def body(tile_values, tile_coords, tile_counts, restrict_basis, prolong_basis, row_partner, col_partner):
    f32 = jnp.float32
    dma = pltpu.SemaphoreType.DMA
    any_spec = pl.BlockSpec(memory_space=pl.ANY)
    vmem_spec = pl.BlockSpec(memory_space=pltpu.VMEM)
    smem_spec = pl.BlockSpec(memory_space=pltpu.SMEM)
    return pl.pallas_call(
        kernel,
        out_shape=jax.ShapeDtypeStruct((RB * K // 2, CB * K // 2), f32),
        in_specs=[any_spec, vmem_spec, any_spec, smem_spec, smem_spec, smem_spec, smem_spec],
        out_specs=vmem_spec,
        scratch_shapes=[
            pltpu.VMEM((SLOTS, TB, TB), f32),
            pltpu.VMEM((4, 2, TB // 2, K), f32),
            pltpu.VMEM((4, 4, K, TB // 4), f32),
            pltpu.VMEM((RB * CB, TB, K), f32),
            pltpu.VMEM((CH, N_ROW, 2, SL, K), f32),
            pltpu.VMEM((CH, N_ROW, 2, SL, K), f32),
            *[pltpu.VMEM((N_ROW, 2, SL, K), f32)] * CH,
            pltpu.VMEM((CH, N_ROW, 2, SL, K), f32),
            pltpu.VMEM((CH, N_ROW, 2, SL, K), f32),
            pltpu.VMEM((2, N_COL, SL, K), f32),
            *[pltpu.VMEM((N_COL, SL, K), f32)] * 2,
            pltpu.VMEM((2, N_COL, SL, K), f32),
            pltpu.VMEM((2, N_COL, SL, K), f32),
            pltpu.SMEM((RB * CB,), jnp.int32),
            pltpu.SMEM((RB * CB,), jnp.int32),
            dma,
            dma,
            dma((4,)),
            dma((3,)),
            dma((4, 2)),
            dma((12,)),
            dma((4, 4)),
            dma((CH,)),
            dma((CH,)),
            dma((CH,)),
            dma((CH,)),
            dma((2,)),
            dma((2,)),
            dma((2,)),
            dma((2,)),
        ],
        compiler_params=pltpu.CompilerParams(collective_id=0, has_side_effects=True, vmem_limit_bytes=60 << 20),
    )(tile_values, restrict_basis, prolong_basis, tile_coords, tile_counts, row_partner, col_partner)


def solution(mesh):
    in_specs = (
        P(("row", "col"), None, None),
        P(("row", "col"), None),
        P(("row", "col")),
        P(("row", "col"), None),
        P(("col", "row"), None),
        P(),
        P(),
    )
    return jax.shard_map(body, mesh=mesh, in_specs=in_specs, out_specs=P("row", "col"), check_vma=False)
```

time: 452 us -> 85.9 us (0.19)
  waiting for transfers between devices: 269 us -> 0 us
  matrix products: 83.4 us -> 0 us
  Pallas kernels: 0 us -> 80.1 us
  loops' own time: 54.4 us -> 0 us
  between operations: 15.8 us -> 0.66 us
  other arithmetic: 11.4 us -> 0 us
  local copies, waits for them, and re-layouts: 15.9 us -> 4.96 us
    all_gather x4 -> x0, waiting for transfers between devices: 268 us -> none  [the longest x1 110 us: body(): gathered = lax.all_gather(given, 'col', axis=1, tiled=True)]
    dot_general x32 -> x0, matrix products: 83.4 us -> none  [the longest x16 45.9 us: add_slot(): product = jnp.dot(left.T, applied, precision=lax.Precision.HIGHEST)]
    pallas_call x0 -> x1, Pallas kernels: none -> 80.1 us  [body(): pl.pallas_call(kernel, out_shape=jax.ShapeDtypeStruct((RB * K // 2, CB *...]
    another operation x1 -> x0, loops' own time: 54.4 us -> none  [body(): local_grid = lax.fori_loop(0, tile_values.shape[0], add_slot, start_grid)]
    dynamic_slice x18 -> x0, local copies, waits for them, and re-layouts: 13.4 us -> none  [the longest x16 10.7 us: add_slot(): block_col = tile_coords[slot_index, 1]]
    add x2 -> x0, other arithmetic: 6.08 us -> none  [the longest x1 3.53 us: body(): row_section = kept + incoming]
    select_n x2 -> x0, other arithmetic: 5.3 us -> none  [pick_half(): given = jnp.where(keep_flag, first, second)]
    unnamed x2 -> x3, local copies, waits for them, and re-layouts: 0.01 us -> 4.96 us
  transfers between devices with their start and end apart: 4 -> 0, of which waited for: 4 -> 0; matrix products, arithmetic and copies ran while one was open for 1% -> 0% of each run, Pallas kernels for 0% -> 0%
where the time goes in v1:
time: 85.9 us; the launch traced here: 85.7 us
  Pallas kernels  80.1 us (93%)
  local copies, waits for them, and re-layouts  4.96 us (6%)
    pallas_call x1, Pallas kernels, body(): pl.pallas_call(kernel, out_shape=jax.ShapeDtypeStruct((RB * K // 2, CB *...  80.1 us
    unnamed x3, local copies, waits for them, and re-layouts  4.96 us

profile of v1, /device:TPU:1, one launch (start us, length us, event | category | flops | bytes accessed | tf_op | source)
XLA Modules:
  0.0 85.7 jit_solution(7888351617100859861)
XLA Ops:
  0.7 1.4 %copy.8.coords = s32[16,2]{1,0:T(8,128)} copy(s32[16,2]{0,1:T(2,128)} %param.8) | data formatting | bytes 256 | tf_op args[1]
  2.0 1.3 %copy.9.row_partner = s32[16,8]{1,0:T(8,128)} copy(s32[16,8]{0,1:T(8,128)} %param.12) | data formatting | bytes 1024 | tf_op args[5]
  3.4 80.1 %shard_map.73 = f32[512,512]{1,0:T(8,128)} custom-call(f32[16,512,512]{2,1,0:T(8,128)} %tiles_hbm.1, f32[128,256]{1,0:T(8,128)} %q_ref.1, f32[256,256]{1,0:T(8,128)} %p_hbm.1, s32[16,2]{1,0:T(8,128)} %copy.8.coords, s32[1]{0:T(128)S(6)} %copy.11.counts, s32[16,8]{1,0:T(8,128)} %copy.9.row_partner, s32[8,16]{1,0:T(8,128)} %col_partner.1), custom_call_target="tpu_custom_call" | custom-call | tf_op jit(solution)/shard_map/pallas_call | solution.py:344
  83.4 2.3 %copy.12 = f32[512,512]{1,0:T(8,128)} copy(f32[512,512]{1,0:T(8,128)} %shard_map.73) | data formatting | bytes 2097152

commit v2 on v1

--- a/solution.py
+++ b/solution.py
@@ -29,7 +29,7 @@
 
 def kernel(
     tiles_hbm,
-    q_ref,
+    q_hbm,
     p_hbm,
     coords,
     counts,
@@ -37,6 +37,7 @@
     col_partner,
     out_ref,
     tiles,
+    qin,
     pbuf,
     qt,
     ubuf,
@@ -57,11 +58,13 @@
     live_sm,
     tile_sem,
     own_sem,
+    q_own_sem,
     p_send,
-    p_fsend,
     p_recv,
     q_send,
-    q_recv,
+    q1_recv,
+    q2_recv,
+    q3_recv,
     s1_send,
     s1_recv,
     s2_send,
@@ -78,11 +81,6 @@
     z, core = r // 2, r % 2
     x, y = c // 4, c % 4
 
-    tile_cp = pltpu.make_async_copy(tiles_hbm, tiles, tile_sem)
-    tile_cp.start()
-    own_cp = pltpu.make_async_copy(p_hbm, pbuf.at[z, core], own_sem)
-    own_cp.start()
-
     z_peers = [((z + dz) % 4) * 2 + (core + dc) % 2 for dz, dc in Z_PEERS]
     xy_peers = [((x + dx) % 4) * 4 + (y + dy) % 4 for dx, dy in XY_PEERS]
 
@@ -92,87 +90,109 @@
     for peer in xy_peers:
         pl.semaphore_signal(barrier, inc=1, device_id={"col": peer}, device_id_type=MESH)
 
-    qt[x, y] = q_ref[...].T
-
-    for pos in range(RB * CB):
+    own_cp = pltpu.make_async_copy(p_hbm, pbuf.at[z, core], own_sem)
+    own_cp.start()
+    q_cp = pltpu.make_async_copy(q_hbm, qin, q_own_sem)
+    q_cp.start()
+    tile_cp = pltpu.make_async_copy(tiles_hbm, tiles, tile_sem)
+    tile_cp.start()
+
+    q_cp.wait()
+    qt[x, y] = qin[...].T
+    own_cp.wait()
+
+    def find_slot(pos, carry):
         slot = jnp.int32(0)
         for s in range(SLOTS):
-            hit = coords[s, 0] * CB + coords[s, 1] == pos
+            hit = coords[0, s] * CB + coords[1, s] == pos
             slot = jnp.where(hit, jnp.int32(s), slot)
         slot_sm[pos] = slot
         live_sm[pos] = jnp.where(slot < counts[0], jnp.int32(1), jnp.int32(0))
+        return carry
 
     pl.semaphore_wait(barrier, len(z_peers) + len(xy_peers))
 
+    up, down, far = lambda v: (v + 1) % 4, lambda v: (v + 3) % 4, lambda v: (v + 2) % 4
+    hb = TB // 4
     sibling = z * 2 + (1 - core)
+
     p_cps = []
-    for n, dz in enumerate((1, 3, 2)):
+
+    def p_half(zs, cs_, h):
+        return pbuf.at[zs, cs_, pl.ds(h * hb, hb)]
+
+    def p_send_to(zs, h, row):
+        n = len(p_cps)
         cp = pltpu.make_async_remote_copy(
-            src_ref=p_hbm,
-            dst_ref=pbuf.at[z, core],
+            src_ref=p_half(zs, core, h),
+            dst_ref=p_half(zs, core, h),
             send_sem=p_send.at[n],
-            recv_sem=p_recv.at[z, core],
-            device_id={"row": ((z + dz) % 4) * 2 + core},
+            recv_sem=p_recv.at[zs, core, h],
+            device_id={"row": row},
             device_id_type=MESH,
         )
         cp.start()
         p_cps.append(cp)
-    cp = pltpu.make_async_remote_copy(
-        src_ref=p_hbm,
-        dst_ref=pbuf.at[z, core],
-        send_sem=p_send.at[3],
-        recv_sem=p_recv.at[z, core],
-        device_id={"row": sibling},
-        device_id_type=MESH,
-    )
-    cp.start()
-    p_cps.append(cp)
-
-    def q_copy(ref, n, recv, dest):
-        return pltpu.make_async_remote_copy(
-            src_ref=ref,
-            dst_ref=ref,
-            send_sem=q_send.at[n],
-            recv_sem=recv,
+
+    def p_wait(zs, cs_, h):
+        view = p_half(zs, cs_, h)
+        pltpu.make_async_copy(view, view, p_recv.at[zs, cs_, h]).wait()
+
+    z_up, z_down = up(z) * 2 + core, down(z) * 2 + core
+
+    q_cps = []
+
+    def q_ref_of(kind, i, j, lo, n):
+        xs, ys = (i, j) if kind == 0 else (j, i)
+        return qt.at[xs, ys, pl.ds(kind * 128 + lo, n)]
+
+    me_i, me_j = (x, y), (y, x)
+
+    def q_dest(kind, i, j):
+        return i * 4 + j if kind == 0 else j * 4 + i
+
+    def q_send_to(kind, i, j, lo, n, sem, dest):
+        cp = pltpu.make_async_remote_copy(
+            src_ref=q_ref_of(kind, i, j, lo, n),
+            dst_ref=q_ref_of(kind, i, j, lo, n),
+            send_sem=q_send.at[len(q_cps)],
+            recv_sem=sem,
             device_id={"col": dest},
             device_id_type=MESH,
         )
-
-    half = K // 2
-    q_cps = []
-    for n, d in enumerate((1, 3, 2)):
-        cp = q_copy(qt.at[x, y, pl.ds(0, half)], n, q_recv.at[0, x], ((x + d) % 4) * 4 + y)
         cp.start()
         q_cps.append(cp)
-        cp = q_copy(qt.at[x, y, pl.ds(half, half)], 3 + n, q_recv.at[1, y], x * 4 + (y + d) % 4)
-        cp.start()
-        q_cps.append(cp)
-    for d in (1, 3, 2):
-        xs, ys = (x + d) % 4, (y + d) % 4
-        q_copy(qt.at[xs, y, pl.ds(0, half)], 0, q_recv.at[0, xs], c).wait_recv()
-        q_copy(qt.at[x, ys, pl.ds(half, half)], 0, q_recv.at[1, ys], c).wait_recv()
-    for n, d in enumerate((1, 3, 2)):
-        cp = q_copy(qt.at[:, y, pl.ds(0, half)], 6 + n, q_recv.at[2, y], x * 4 + (y + d) % 4)
-        cp.start()
-        q_cps.append(cp)
-        cp = q_copy(qt.at[x, :, pl.ds(half, half)], 9 + n, q_recv.at[3, x], ((x + d) % 4) * 4 + y)
-        cp.start()
-        q_cps.append(cp)
-
-    def p_wait(zs, cs_):
-        pltpu.make_async_copy(pbuf.at[zs, cs_], pbuf.at[zs, cs_], p_recv.at[zs, cs_]).wait()
-
-    def p_forward(n, zs):
-        cp = pltpu.make_async_remote_copy(
-            src_ref=pbuf.at[zs, core],
-            dst_ref=pbuf.at[zs, core],
-            send_sem=p_fsend.at[n],
-            recv_sem=p_recv.at[zs, core],
-            device_id={"row": sibling},
-            device_id_type=MESH,
-        )
-        cp.start()
-        p_cps.append(cp)
+
+    def q_wait(kind, i, j, lo, n, sem):
+        view = q_ref_of(kind, i, j, lo, n)
+        pltpu.make_async_copy(view, view, sem).wait()
+
+    def q_first(kind):
+        i, j = me_i[kind], me_j[kind]
+        for step in (up, down, far):
+            q_send_to(kind, i, j, 0, 128, q1_recv.at[kind, i], q_dest(kind, step(i), j))
+
+    def q_second(kind, i):
+        mi, j = me_i[kind], me_j[kind]
+        for step in (up, down):
+            q_send_to(kind, i, j, 0, 128, q2_recv.at[kind, i, j], q_dest(kind, mi, step(j)))
+
+    def q_take1(kind, step):
+        i, j = step(me_i[kind]), me_j[kind]
+        q_wait(kind, i, j, 0, 128, q1_recv.at[kind, i])
+        q_second(kind, i)
+
+    def q_take2(kind, i):
+        mi, j = me_i[kind], me_j[kind]
+        q_wait(kind, i, down(j), 0, 128, q2_recv.at[kind, i, down(j)])
+        q_send_to(kind, i, down(j), 0, 64, q3_recv.at[kind, i, 0], q_dest(kind, mi, up(j)))
+        q_wait(kind, i, up(j), 0, 128, q2_recv.at[kind, i, up(j)])
+        q_send_to(kind, i, up(j), 64, 64, q3_recv.at[kind, i, 1], q_dest(kind, mi, down(j)))
+
+    def q_take3(kind, i):
+        j = far(me_j[kind])
+        q_wait(kind, i, j, 0, 64, q3_recv.at[kind, i, 0])
+        q_wait(kind, i, j, 64, 64, q3_recv.at[kind, i, 1])
 
     def apply_block(b):
         def one(a, carry):
@@ -184,30 +204,71 @@
 
         lax.fori_loop(0, RB, one, 0)
 
-    own_cp.wait()
-    p_wait(z, 1 - core)
+    def apply_half(b, cs_, first):
+        def one(a, carry):
+            pos = a * CB + b
+            cols = pl.ds(pl.multiple_of(cs_ * (TB // 2), TB // 2), TB // 2)
+            tile = tiles[slot_sm[pos], :, cols]
+            u = jnp.dot(tile, pbuf[b, cs_], precision=HIGH, preferred_element_type=jnp.float32)
+            ubuf[pos] = u if first else ubuf[pos] + u
+            return carry
+
+        lax.fori_loop(0, RB, one, 0)
+
+    for h in (0, 1):
+        p_send_to(z, h, z_up)
+        p_send_to(z, 1 - h, z_down)
+    for kind in (0, 1):
+        q_first(kind)
+    for h in (0, 1):
+        p_send_to(z, h, sibling)
+    for kind in (0, 1):
+        q_second(kind, me_i[kind])
+    lax.fori_loop(0, RB * CB, find_slot, 0)
+    for step in (up, down):
+        for kind in (0, 1):
+            q_take1(kind, step)
+    for h in (0, 1):
+        p_wait(z, 1 - core, h)
     tile_cp.wait()
+    for kind in (0, 1):
+        q_take1(kind, far)
+    p_wait(down(z), core, 0)
+    p_send_to(down(z), 0, z_up)
+    p_wait(up(z), core, 1)
+    p_send_to(up(z), 1, z_down)
+    p_send_to(down(z), 0, sibling)
+    p_send_to(up(z), 1, sibling)
     apply_block(z)
-    for n, d in enumerate((1, 3)):
-        zs = (z + d) % 4
-        p_wait(zs, core)
-        p_forward(n, zs)
-    for d in (1, 3):
-        zs = (z + d) % 4
-        p_wait(zs, 1 - core)
-        apply_block(zs)
-    zs = (z + 2) % 4
-    p_wait(zs, core)
-    p_forward(2, zs)
-    p_wait(zs, 1 - core)
-    apply_block(zs)
-
-    for d in (1, 3, 2):
-        xs, ys = (x + d) % 4, (y + d) % 4
-        q_copy(qt.at[:, ys, pl.ds(0, half)], 0, q_recv.at[2, ys], c).wait_recv()
-        q_copy(qt.at[xs, :, pl.ds(half, half)], 0, q_recv.at[3, xs], c).wait_recv()
-
-    my_rp = row_partner[c, r]
+    for kind in (0, 1):
+        q_take2(kind, me_i[kind])
+    p_wait(down(z), core, 1)
+    p_send_to(down(z), 1, sibling)
+    p_wait(up(z), core, 0)
+    p_send_to(up(z), 0, sibling)
+    for step in (up, down):
+        for kind in (0, 1):
+            q_take2(kind, step(me_i[kind]))
+    for h in (0, 1):
+        p_wait(down(z), 1 - core, h)
+    apply_block(down(z))
+    for kind in (0, 1):
+        q_take2(kind, far(me_i[kind]))
+    for h in (0, 1):
+        p_wait(far(z), core, h)
+        p_send_to(far(z), h, sibling)
+    for h in (0, 1):
+        p_wait(up(z), 1 - core, h)
+    apply_block(up(z))
+    apply_half(far(z), core, True)
+    for h in (0, 1):
+        p_wait(far(z), 1 - core, h)
+    apply_half(far(z), 1 - core, False)
+    for kind in (0, 1):
+        for step in (lambda v: v, up, down, far):
+            q_take3(kind, step(me_i[kind]))
+
+    my_rp = row_partner[r, c]
     my_cp = col_partner[r, c]
     my_h = jnp.where(r > my_rp, jnp.int32(1), jnp.int32(0))
     my_g = jnp.where(c > my_cp, jnp.int32(1), jnp.int32(0))
@@ -217,15 +278,14 @@
         a = 2 * row_half + ch % 2
         col_half = (1 - keep_col) if ch < 2 else keep_col
 
-        def one(n, carry):
-            pos = a * CB + 2 * col_half + n
-            left = jnp.concatenate([qt[a, i] for i in range(4)], axis=1)
-            g = jnp.dot(left, ubuf[pos], precision=HIGH, preferred_element_type=jnp.float32)
-            g = jnp.where(live_sm[pos] > 0, g, jnp.zeros_like(g))
-            dst[ch, :, n] = g.reshape(N_ROW, SL, K)
-            return carry
-
-        lax.fori_loop(0, 2, one, 0)
+        pos = a * CB + 2 * col_half
+        left = jnp.concatenate([qt[a, i] for i in range(4)], axis=1)
+        right = jnp.concatenate([ubuf[pos], ubuf[pos + 1]], axis=1)
+        g = jnp.dot(left, right, precision=HIGH, preferred_element_type=jnp.float32)
+        for n in range(2):
+            gn = g[:, n * K : (n + 1) * K]
+            gn = jnp.where(live_sm[pos + n] > 0, gn, jnp.zeros_like(gn))
+            dst[ch, :, n] = gn.reshape(N_ROW, SL, K)
 
     def send1(ch):
         recv1[ch][r] = gv[ch, r]
@@ -247,7 +307,7 @@
         take(recv1[ch], N_ROW - 1, s1_recv.at[ch])
 
         def one(k, carry):
-            snd2[ch, k] = recv1[ch][row_partner[c, k]]
+            snd2[ch, k] = recv1[ch][row_partner[k, c]]
             return carry
 
         lax.fori_loop(0, N_ROW, one, 0)
@@ -344,10 +404,11 @@
     return pl.pallas_call(
         kernel,
         out_shape=jax.ShapeDtypeStruct((RB * K // 2, CB * K // 2), f32),
-        in_specs=[any_spec, vmem_spec, any_spec, smem_spec, smem_spec, smem_spec, smem_spec],
+        in_specs=[any_spec, any_spec, any_spec, smem_spec, smem_spec, smem_spec, smem_spec],
         out_specs=vmem_spec,
         scratch_shapes=[
             pltpu.VMEM((SLOTS, TB, TB), f32),
+            pltpu.VMEM((TB // 4, K), f32),
             pltpu.VMEM((4, 2, TB // 2, K), f32),
             pltpu.VMEM((4, 4, K, TB // 4), f32),
             pltpu.VMEM((RB * CB, TB, K), f32),
@@ -364,11 +425,13 @@
             pltpu.SMEM((RB * CB,), jnp.int32),
             dma,
             dma,
-            dma((4,)),
-            dma((3,)),
-            dma((4, 2)),
-            dma((12,)),
-            dma((4, 4)),
+            dma,
+            dma((14,)),
+            dma((4, 2, 2)),
+            dma((38,)),
+            dma((2, 4)),
+            dma((2, 4, 4)),
+            dma((2, 4, 2)),
             dma((CH,)),
             dma((CH,)),
             dma((CH,)),
@@ -379,7 +442,7 @@
             dma((2,)),
         ],
         compiler_params=pltpu.CompilerParams(collective_id=0, has_side_effects=True, vmem_limit_bytes=60 << 20),
-    )(tile_values, restrict_basis, prolong_basis, tile_coords, tile_counts, row_partner, col_partner)
+    )(tile_values, restrict_basis, prolong_basis, tile_coords.T, tile_counts, row_partner.T, col_partner)
 
 
 def solution(mesh):

time: 85.9 us -> 81.2 us (0.945)
  local copies, waits for them, and re-layouts: 4.96 us -> 2.26 us
  Pallas kernels: 80.1 us -> 78.1 us
    unnamed x3 -> x1, local copies, waits for them, and re-layouts: 4.96 us -> 2.26 us
    pallas_call x1, Pallas kernels: 80.1 us -> 78.1 us  [body(): pl.pallas_call(kernel, out_shape=jax.ShapeDtypeStruct((RB * K // 2, CB *...]
where the time goes in v2:
time: 81.2 us; the launch traced here: 81 us
  Pallas kernels  78.1 us (96%)
  local copies, waits for them, and re-layouts  2.26 us (3%)
    pallas_call x1, Pallas kernels, body(): pl.pallas_call(kernel, out_shape=jax.ShapeDtypeStruct((RB * K // 2, CB *...  78.1 us
    unnamed x1, local copies, waits for them, and re-layouts  2.26 us

profile of v2, /device:TPU:1, one launch (start us, length us, event | category | flops | bytes accessed | tf_op | source)
XLA Modules:
  0.0 81.0 jit_solution(7194514606773583952)
XLA Ops:
  0.7 78.1 %shard_map.73 = f32[512,512]{1,0:T(8,128)} custom-call(f32[16,512,512]{2,1,0:T(8,128)} %tiles_hbm.1, f32[128,256]{1,0:T(8,128)} %q_hbm.1, f32[256,256]{1,0:T(8,128)} %p_hbm.1, s32[2,16]{1,0:T(2,128)} %bitcast.3, s32[1]{0:T(128)S(6)} %copy.9.counts, s32[8,16]{1,0:T(8,128)} %bitcast.2, s32[8,16]{1,0:T(8,128)} %col_partner.1), custom_call_target="tpu_custom_call" | custom-call | tf_op jit(solution)/shard_map/pallas_call | solution.py:404
  78.7 2.3 %copy.10 = f32[512,512]{1,0:T(8,128)} copy(f32[512,512]{1,0:T(8,128)} %shard_map.73) | data formatting | bytes 2097152

commit v3 on v2

--- a/solution.py
+++ b/solution.py
@@ -54,6 +54,10 @@
     crecv_1,
     csnd2,
     cinc,
+    cz1,
+    cz1_in,
+    cz2,
+    cz2_in,
     slot_sm,
     live_sm,
     tile_sem,
@@ -73,6 +77,8 @@
     x1_recv,
     x2_send,
     x2_recv,
+    c_send,
+    c_recv,
 ):
     recv1 = (recv1_0, recv1_1, recv1_2, recv1_3)
     crecv = (crecv_0, crecv_1)
@@ -303,14 +309,7 @@
         view = ref.at[pl.ds(0, n)]
         pltpu.make_async_copy(view, view, sem).wait()
 
-    def send2(ch):
-        take(recv1[ch], N_ROW - 1, s1_recv.at[ch])
-
-        def one(k, carry):
-            snd2[ch, k] = recv1[ch][row_partner[k, c]]
-            return carry
-
-        lax.fori_loop(0, N_ROW, one, 0)
+    def row_send2(ch):
         inc[ch, r] = snd2[ch, r]
         for peer in z_peers:
             pltpu.make_async_remote_copy(
@@ -322,9 +321,22 @@
                 device_id_type=MESH,
             ).start()
 
+    def send2(ch):
+        take(recv1[ch], N_ROW - 1, s1_recv.at[ch])
+
+        def one(k, carry):
+            snd2[ch, k] = recv1[ch][row_partner[k, c]]
+            return carry
+
+        lax.fori_loop(0, N_ROW, one, 0)
+        row_send2(ch)
+
     def cross1(ch):
-        take(inc.at[ch], N_ROW - 1, s2_recv.at[ch])
-        cs[ch] = (kept[ch] + inc[ch]).reshape(N_COL, SL, K)
+        if ch == 0:
+            cs[ch] = kept[ch].reshape(N_COL, SL, K)
+        else:
+            take(inc.at[ch], N_ROW - 1, s2_recv.at[ch])
+            cs[ch] = (kept[ch] + inc[ch]).reshape(N_COL, SL, K)
         crecv[ch][c] = cs[ch, c]
         for peer in xy_peers:
             pltpu.make_async_remote_copy(
@@ -335,6 +347,56 @@
                 device_id={"col": peer},
                 device_id_type=MESH,
             ).start()
+
+    parts = [(m, slice(i * 8, i * 8 + 8), slice(j * 128, j * 128 + 128)) for m in range(2) for i in range(4) for j in range(2)]
+
+    def slice_send(src, dst, n):
+        dst[c] = src[c]
+        for peer in xy_peers:
+            pltpu.make_async_remote_copy(
+                src_ref=src.at[peer],
+                dst_ref=dst.at[c],
+                send_sem=c_send.at[n],
+                recv_sem=c_recv.at[n],
+                device_id={"col": peer},
+                device_id_type=MESH,
+            ).start()
+
+    def slices1():
+        take(recv1[0], N_ROW - 1, s1_recv.at[0])
+
+        def one(k, carry):
+            value = recv1[0][row_partner[k, c]]
+            for n, (m, rows, cols) in enumerate(parts):
+                cz1[n, k] = value[m, rows, cols]
+            return carry
+
+        lax.fori_loop(0, N_ROW, one, 0)
+        slice_send(cz1, cz1_in, 0)
+
+    def slices2():
+        take(cz1_in, N_COL - 1, c_recv.at[0])
+
+        def one(n, carry):
+            for k in range(N_ROW):
+                cz2[n, k] = cz1_in[col_partner[k, n], k]
+            return carry
+
+        lax.fori_loop(0, N_COL, one, 0)
+        slice_send(cz2, cz2_in, 1)
+
+    def combine():
+        take(cz2_in, N_COL - 1, c_recv.at[1])
+        take(recv1[2], N_ROW - 1, s1_recv.at[2])
+
+        def one(k, carry):
+            value = recv1[2][row_partner[k, c]]
+            for n, (m, rows, cols) in enumerate(parts):
+                snd2[2, k, m, rows, cols] = value[m, rows, cols] + cz2_in[n, k]
+            return carry
+
+        lax.fori_loop(0, N_ROW, one, 0)
+        row_send2(2)
 
     def cross2(ch):
         take(crecv[ch], N_COL - 1, x1_recv.at[ch])
@@ -364,22 +426,21 @@
             out_ref[a * K : (a + 1) * K, n * K : (n + 1) * K] = total.reshape(K, K)
 
     given_h = 1 - my_h
-    blocks(gv, 0, given_h, partner_g)
-    send1(0)
-    blocks(gv, 1, given_h, partner_g)
-    send1(1)
-    blocks(gv, 2, given_h, partner_g)
+    for ch in range(3):
+        blocks(gv, ch, given_h, partner_g)
+        send1(ch)
+    blocks(kept, 0, my_h, my_g)
+    cross1(0)
     blocks(gv, 3, given_h, partner_g)
-    for ch in range(CH):
+    for ch in range(1, CH):
         blocks(kept, ch, my_h, my_g)
-    send2(0)
+    slices1()
     send2(1)
-    send1(2)
     send1(3)
-    cross1(0)
+    cross2(0)
+    slices2()
     cross1(1)
-    cross2(0)
-    send2(2)
+    combine()
     cross2(1)
     send2(3)
     finish(0)
@@ -389,10 +450,12 @@
         cp.wait_send()
     for ch in range(CH):
         take(gv.at[ch], N_ROW - 1, s1_send.at[ch])
-        take(snd2.at[ch], N_ROW - 1, s2_send.at[ch])
+        if ch > 0:
+            take(snd2.at[ch], N_ROW - 1, s2_send.at[ch])
     for ch in range(2):
         take(cs.at[ch], N_COL - 1, x1_send.at[ch])
         take(csnd2.at[ch], N_COL - 1, x2_send.at[ch])
+        take((cz1, cz2)[ch], N_COL - 1, c_send.at[ch])
 
 
 def body(tile_values, tile_coords, tile_counts, restrict_basis, prolong_basis, row_partner, col_partner):
@@ -421,6 +484,7 @@
             *[pltpu.VMEM((N_COL, SL, K), f32)] * 2,
             pltpu.VMEM((2, N_COL, SL, K), f32),
             pltpu.VMEM((2, N_COL, SL, K), f32),
+            *[pltpu.VMEM((N_COL, N_ROW, 8, 128), f32)] * 4,
             pltpu.SMEM((RB * CB,), jnp.int32),
             pltpu.SMEM((RB * CB,), jnp.int32),
             dma,
@@ -440,6 +504,8 @@
             dma((2,)),
             dma((2,)),
             dma((2,)),
+            dma((2,)),
+            dma((2,)),
         ],
         compiler_params=pltpu.CompilerParams(collective_id=0, has_side_effects=True, vmem_limit_bytes=60 << 20),
     )(tile_values, restrict_basis, prolong_basis, tile_coords.T, tile_counts, row_partner.T, col_partner)

time: 81.2 us -> 77.6 us (0.956)
  Pallas kernels: 78.1 us -> 74.5 us
    pallas_call x1, Pallas kernels: 78.1 us -> 74.5 us  [body(): pl.pallas_call(kernel, out_shape=jax.ShapeDtypeStruct((RB * K // 2, CB *...]
where the time goes in v3:
time: 77.6 us; the launch traced here: 77.4 us
  Pallas kernels  74.5 us (96%)
  local copies, waits for them, and re-layouts  2.26 us (3%)
    pallas_call x1, Pallas kernels, body(): pl.pallas_call(kernel, out_shape=jax.ShapeDtypeStruct((RB * K // 2, CB *...  74.5 us
    unnamed x1, local copies, waits for them, and re-layouts  2.26 us

profile of v3, /device:TPU:1, one launch (start us, length us, event | category | flops | bytes accessed | tf_op | source)
XLA Modules:
  0.0 77.4 jit_solution(4562301415796056062)
XLA Ops:
  0.7 74.5 %shard_map.73 = f32[512,512]{1,0:T(8,128)} custom-call(f32[16,512,512]{2,1,0:T(8,128)} %tiles_hbm.1, f32[128,256]{1,0:T(8,128)} %q_hbm.1, f32[256,256]{1,0:T(8,128)} %p_hbm.1, s32[2,16]{1,0:T(2,128)} %bitcast.3, s32[1]{0:T(128)S(6)} %copy.9.counts, s32[8,16]{1,0:T(8,128)} %bitcast.2, s32[8,16]{1,0:T(8,128)} %col_partner.1), custom_call_target="tpu_custom_call" | custom-call | tf_op jit(solution)/shard_map/pallas_call | solution.py:467
  75.1 2.3 %copy.10 = f32[512,512]{1,0:T(8,128)} copy(f32[512,512]{1,0:T(8,128)} %shard_map.73) | data formatting | bytes 2097152

commit v4 on v3

--- a/solution.py
+++ b/solution.py
@@ -31,10 +31,11 @@
     tiles_hbm,
     q_hbm,
     p_hbm,
-    coords,
-    counts,
-    row_partner,
-    col_partner,
+    coords_hbm,
+    counts_hbm,
+    row_partner_hbm,
+    col_partner_hbm,
+    out_hbm,
     out_ref,
     tiles,
     qin,
@@ -58,8 +59,13 @@
     cz1_in,
     cz2,
     cz2_in,
+    coords,
+    counts,
+    row_partner,
+    col_partner,
     slot_sm,
     live_sm,
+    table_sem,
     tile_sem,
     own_sem,
     q_own_sem,
@@ -68,7 +74,6 @@
     q_send,
     q1_recv,
     q2_recv,
-    q3_recv,
     s1_send,
     s1_recv,
     s2_send,
@@ -77,6 +82,7 @@
     x1_recv,
     x2_send,
     x2_recv,
+    out_sem,
     c_send,
     c_recv,
 ):
@@ -96,6 +102,16 @@
     for peer in xy_peers:
         pl.semaphore_signal(barrier, inc=1, device_id={"col": peer}, device_id_type=MESH)
 
+    table_cps = []
+    for ref, sm in (
+        (coords_hbm, coords),
+        (counts_hbm, counts),
+        (row_partner_hbm, row_partner),
+        (col_partner_hbm, col_partner),
+    ):
+        cp = pltpu.make_async_copy(ref, sm, table_sem.at[len(table_cps)])
+        cp.start()
+        table_cps.append(cp)
     own_cp = pltpu.make_async_copy(p_hbm, pbuf.at[z, core], own_sem)
     own_cp.start()
     q_cp = pltpu.make_async_copy(q_hbm, qin, q_own_sem)
@@ -116,6 +132,9 @@
         live_sm[pos] = jnp.where(slot < counts[0], jnp.int32(1), jnp.int32(0))
         return carry
 
+    for cp in table_cps:
+        cp.wait()
+    lax.fori_loop(0, RB * CB, find_slot, 0)
     pl.semaphore_wait(barrier, len(z_peers) + len(xy_peers))
 
     up, down, far = lambda v: (v + 1) % 4, lambda v: (v + 3) % 4, lambda v: (v + 2) % 4
@@ -180,7 +199,7 @@
 
     def q_second(kind, i):
         mi, j = me_i[kind], me_j[kind]
-        for step in (up, down):
+        for step in (up, down, far):
             q_send_to(kind, i, j, 0, 128, q2_recv.at[kind, i, j], q_dest(kind, mi, step(j)))
 
     def q_take1(kind, step):
@@ -189,18 +208,11 @@
         q_second(kind, i)
 
     def q_take2(kind, i):
-        mi, j = me_i[kind], me_j[kind]
-        q_wait(kind, i, down(j), 0, 128, q2_recv.at[kind, i, down(j)])
-        q_send_to(kind, i, down(j), 0, 64, q3_recv.at[kind, i, 0], q_dest(kind, mi, up(j)))
-        q_wait(kind, i, up(j), 0, 128, q2_recv.at[kind, i, up(j)])
-        q_send_to(kind, i, up(j), 64, 64, q3_recv.at[kind, i, 1], q_dest(kind, mi, down(j)))
-
-    def q_take3(kind, i):
-        j = far(me_j[kind])
-        q_wait(kind, i, j, 0, 64, q3_recv.at[kind, i, 0])
-        q_wait(kind, i, j, 64, 64, q3_recv.at[kind, i, 1])
-
-    def apply_block(b):
+        for step in (up, down, far):
+            j = step(me_j[kind])
+            q_wait(kind, i, j, 0, 128, q2_recv.at[kind, i, j])
+
+    def apply_block(b, lo=0, hi=RB):
         def one(a, carry):
             right = pbuf[b].reshape(TB, K)
             pos = a * CB + b
@@ -208,7 +220,7 @@
             ubuf[pos] = jnp.dot(tile, right, precision=HIGH, preferred_element_type=jnp.float32)
             return carry
 
-        lax.fori_loop(0, RB, one, 0)
+        lax.fori_loop(lo, hi, one, 0)
 
     def apply_half(b, cs_, first):
         def one(a, carry):
@@ -230,7 +242,6 @@
         p_send_to(z, h, sibling)
     for kind in (0, 1):
         q_second(kind, me_i[kind])
-    lax.fori_loop(0, RB * CB, find_slot, 0)
     for step in (up, down):
         for kind in (0, 1):
             q_take1(kind, step)
@@ -246,33 +257,27 @@
     p_send_to(down(z), 0, sibling)
     p_send_to(up(z), 1, sibling)
     apply_block(z)
-    for kind in (0, 1):
-        q_take2(kind, me_i[kind])
     p_wait(down(z), core, 1)
     p_send_to(down(z), 1, sibling)
     p_wait(up(z), core, 0)
     p_send_to(up(z), 0, sibling)
-    for step in (up, down):
-        for kind in (0, 1):
-            q_take2(kind, step(me_i[kind]))
     for h in (0, 1):
         p_wait(down(z), 1 - core, h)
     apply_block(down(z))
-    for kind in (0, 1):
-        q_take2(kind, far(me_i[kind]))
+    for h in (0, 1):
+        p_wait(up(z), 1 - core, h)
+    apply_block(up(z), 0, 1)
     for h in (0, 1):
         p_wait(far(z), core, h)
         p_send_to(far(z), h, sibling)
-    for h in (0, 1):
-        p_wait(up(z), 1 - core, h)
-    apply_block(up(z))
+    apply_block(up(z), 1, RB)
     apply_half(far(z), core, True)
     for h in (0, 1):
         p_wait(far(z), 1 - core, h)
     apply_half(far(z), 1 - core, False)
     for kind in (0, 1):
         for step in (lambda v: v, up, down, far):
-            q_take3(kind, step(me_i[kind]))
+            q_take2(kind, step(me_i[kind]))
 
     my_rp = row_partner[r, c]
     my_cp = col_partner[r, c]
@@ -424,6 +429,10 @@
             total = kept[2 + a, :, n] + inc[2 + a, :, n]
             total = total + cinc[a].reshape(N_ROW, 2, SL, K)[:, n]
             out_ref[a * K : (a + 1) * K, n * K : (n + 1) * K] = total.reshape(K, K)
+        rows = pl.ds(a * K, K)
+        cp = pltpu.make_async_copy(out_ref.at[rows], out_hbm.at[rows], out_sem.at[a])
+        cp.start()
+        return cp
 
     given_h = 1 - my_h
     for ch in range(3):
@@ -443,9 +452,10 @@
     combine()
     cross2(1)
     send2(3)
-    finish(0)
-    finish(1)
-
+    out_cps = [finish(0), finish(1)]
+
+    for cp in out_cps:
+        cp.wait()
     for cp in p_cps + q_cps:
         cp.wait_send()
     for ch in range(CH):
@@ -462,14 +472,13 @@
     f32 = jnp.float32
     dma = pltpu.SemaphoreType.DMA
     any_spec = pl.BlockSpec(memory_space=pl.ANY)
-    vmem_spec = pl.BlockSpec(memory_space=pltpu.VMEM)
-    smem_spec = pl.BlockSpec(memory_space=pltpu.SMEM)
     return pl.pallas_call(
         kernel,
         out_shape=jax.ShapeDtypeStruct((RB * K // 2, CB * K // 2), f32),
-        in_specs=[any_spec, any_spec, any_spec, smem_spec, smem_spec, smem_spec, smem_spec],
-        out_specs=vmem_spec,
+        in_specs=[any_spec] * 7,
+        out_specs=any_spec,
         scratch_shapes=[
+            pltpu.VMEM((RB * K // 2, CB * K // 2), f32),
             pltpu.VMEM((SLOTS, TB, TB), f32),
             pltpu.VMEM((TB // 4, K), f32),
             pltpu.VMEM((4, 2, TB // 2, K), f32),
@@ -485,21 +494,26 @@
             pltpu.VMEM((2, N_COL, SL, K), f32),
             pltpu.VMEM((2, N_COL, SL, K), f32),
             *[pltpu.VMEM((N_COL, N_ROW, 8, 128), f32)] * 4,
+            pltpu.SMEM((2, SLOTS), jnp.int32),
+            pltpu.SMEM((1,), jnp.int32),
+            pltpu.SMEM((N_ROW, N_COL), jnp.int32),
+            pltpu.SMEM((N_ROW, N_COL), jnp.int32),
             pltpu.SMEM((RB * CB,), jnp.int32),
             pltpu.SMEM((RB * CB,), jnp.int32),
+            dma((4,)),
             dma,
             dma,
             dma,
             dma((14,)),
             dma((4, 2, 2)),
-            dma((38,)),
+            dma((30,)),
             dma((2, 4)),
             dma((2, 4, 4)),
-            dma((2, 4, 2)),
             dma((CH,)),
             dma((CH,)),
             dma((CH,)),
             dma((CH,)),
+            dma((2,)),
             dma((2,)),
             dma((2,)),
             dma((2,)),

time: 77.6 us -> 75.1 us (0.968)
  Pallas kernels: 74.5 us -> 71.6 us
    pallas_call x1, Pallas kernels: 74.5 us -> 71.6 us  [body(): pl.pallas_call(kernel, out_shape=jax.ShapeDtypeStruct((RB * K // 2, CB *...]
where the time goes in v4:
time: 75.1 us; the launch traced here: 74.5 us
  Pallas kernels  71.6 us (95%)
  local copies, waits for them, and re-layouts  2.26 us (3%)
    pallas_call x1, Pallas kernels, body(): pl.pallas_call(kernel, out_shape=jax.ShapeDtypeStruct((RB * K // 2, CB *...  71.6 us
    unnamed x1, local copies, waits for them, and re-layouts  2.26 us

profile of v4, /device:TPU:1, one launch (start us, length us, event | category | flops | bytes accessed | tf_op | source)
XLA Modules:
  0.0 74.5 jit_solution(5960823641867037675)
XLA Ops:
  0.7 71.6 %shard_map.73 = f32[512,512]{1,0:T(8,128)} custom-call(f32[16,512,512]{2,1,0:T(8,128)} %tiles_hbm.1, f32[128,256]{1,0:T(8,128)} %q_hbm.1, f32[256,256]{1,0:T(8,128)} %p_hbm.1, s32[2,16]{1,0:T(2,128)} %bitcast.3, s32[1]{0:T(128)S(6)} %copy.9.counts_hbm, s32[8,16]{1,0:T(8,128)} %bitcast.2, s32[8,16]{1,0:T(8,128)} %col_partner_hbm.1), custom_call_target="tpu_custom_call" | custom-call | tf_op jit(solution)/shard_map/pallas_call | solution.py:475
  72.3 2.3 %copy.10 = f32[512,512]{1,0:T(8,128)} copy(f32[512,512]{1,0:T(8,128)} %shard_map.73) | data formatting | bytes 2097152

commit v5 on v4

--- a/solution.py
+++ b/solution.py
@@ -35,7 +35,6 @@
     counts_hbm,
     row_partner_hbm,
     col_partner_hbm,
-    out_hbm,
     out_ref,
     tiles,
     qin,
@@ -82,7 +81,6 @@
     x1_recv,
     x2_send,
     x2_recv,
-    out_sem,
     c_send,
     c_recv,
 ):
@@ -429,10 +427,6 @@
             total = kept[2 + a, :, n] + inc[2 + a, :, n]
             total = total + cinc[a].reshape(N_ROW, 2, SL, K)[:, n]
             out_ref[a * K : (a + 1) * K, n * K : (n + 1) * K] = total.reshape(K, K)
-        rows = pl.ds(a * K, K)
-        cp = pltpu.make_async_copy(out_ref.at[rows], out_hbm.at[rows], out_sem.at[a])
-        cp.start()
-        return cp
 
     given_h = 1 - my_h
     for ch in range(3):
@@ -452,10 +446,9 @@
     combine()
     cross2(1)
     send2(3)
-    out_cps = [finish(0), finish(1)]
-
-    for cp in out_cps:
-        cp.wait()
+    finish(0)
+    finish(1)
+
     for cp in p_cps + q_cps:
         cp.wait_send()
     for ch in range(CH):
@@ -471,14 +464,14 @@
 def body(tile_values, tile_coords, tile_counts, restrict_basis, prolong_basis, row_partner, col_partner):
     f32 = jnp.float32
     dma = pltpu.SemaphoreType.DMA
-    any_spec = pl.BlockSpec(memory_space=pl.ANY)
     return pl.pallas_call(
         kernel,
         out_shape=jax.ShapeDtypeStruct((RB * K // 2, CB * K // 2), f32),
-        in_specs=[any_spec] * 7,
-        out_specs=any_spec,
+        in_specs=[pl.BlockSpec(memory_space=pltpu.HBM)] * 4
+        + [pl.BlockSpec(memory_space=pl.ANY)]
+        + [pl.BlockSpec(memory_space=pltpu.HBM)] * 2,
+        out_specs=pl.BlockSpec(memory_space=pltpu.VMEM),
         scratch_shapes=[
-            pltpu.VMEM((RB * K // 2, CB * K // 2), f32),
             pltpu.VMEM((SLOTS, TB, TB), f32),
             pltpu.VMEM((TB // 4, K), f32),
             pltpu.VMEM((4, 2, TB // 2, K), f32),
@@ -519,10 +512,22 @@
             dma((2,)),
             dma((2,)),
             dma((2,)),
-            dma((2,)),
         ],
-        compiler_params=pltpu.CompilerParams(collective_id=0, has_side_effects=True, vmem_limit_bytes=60 << 20),
-    )(tile_values, restrict_basis, prolong_basis, tile_coords.T, tile_counts, row_partner.T, col_partner)
+        compiler_params=pltpu.CompilerParams(collective_id=0, has_side_effects=True, vmem_limit_bytes=48 << 20),
+    )(
+        *[
+            value if value.size == 1 else pltpu.with_memory_space_constraint(value, pltpu.HBM)
+            for value in (
+                tile_values,
+                restrict_basis,
+                prolong_basis,
+                tile_coords.T,
+                tile_counts,
+                row_partner.T,
+                col_partner,
+            )
+        ]
+    )
 
 
 def solution(mesh):

time: 75.1 us -> 72.9 us (0.971)
  local copies, waits for them, and re-layouts: 2.26 us -> 0.97 us
  Pallas kernels: 71.6 us -> 70.8 us
    unnamed x1, local copies, waits for them, and re-layouts: 2.26 us -> 0.97 us
    pallas_call x1, Pallas kernels: 71.6 us -> 70.8 us  [body(): pl.pallas_call(kernel, out_shape=jax.ShapeDtypeStruct((RB * K // 2, CB *...]
where the time goes in v5:
time: 72.9 us; the launch traced here: 72.4 us
  Pallas kernels  70.8 us (97%)
  local copies, waits for them, and re-layouts  0.97 us (1%)
    pallas_call x1, Pallas kernels, body(): pl.pallas_call(kernel, out_shape=jax.ShapeDtypeStruct((RB * K // 2, CB *...  70.8 us

profile of v5, /device:TPU:1, one launch (start us, length us, event | category | flops | bytes accessed | tf_op | source)
XLA Modules:
  0.0 72.4 jit_solution(3568814352975576693)
XLA Ops:
  0.7 70.8 %shard_map.73 = f32[512,512]{1,0:T(8,128)S(1)} custom-call(f32[16,512,512]{2,1,0:T(8,128)} %tiles_hbm.1, f32[128,256]{1,0:T(8,128)} %q_hbm.1, f32[256,256]{1,0:T(8,128)} %p_hbm.1, s32[2,16]{1,0:T(2,128)} %bitcast.3, s32[1]{0:T(128)S(6)} %copy.9.counts_hbm, s32[8,16]{1,0:T(8,128)} %bitcast.2, s32[8,16]{1,0:T(8,128)} %col_partner_hbm.1), custom_call_target="tpu_custom_call" | custom-call | tf_op jit(solution)/shard_map/pallas_call | solution.py:467
  71.4 1.0 %copy.10 = f32[512,512]{1,0:T(8,128)} copy(f32[512,512]{1,0:T(8,128)S(1)} %shard_map.73) | data formatting | bytes 2097152

commit v6 on v5

--- a/solution.py
+++ b/solution.py
@@ -438,9 +438,9 @@
     for ch in range(1, CH):
         blocks(kept, ch, my_h, my_g)
     slices1()
+    cross2(0)
     send2(1)
     send1(3)
-    cross2(0)
     slices2()
     cross1(1)
     combine()

time: 72.9 us -> 72.7 us (level)
  no operation moved by 1% of the time
where the time goes in v6:
time: 72.7 us; the launch traced here: 72.3 us
  Pallas kernels  70.7 us (97%)
  local copies, waits for them, and re-layouts  0.97 us (1%)
    pallas_call x1, Pallas kernels, body(): pl.pallas_call(kernel, out_shape=jax.ShapeDtypeStruct((RB * K // 2, CB *...  70.7 us

profile of v6, /device:TPU:1, one launch (start us, length us, event | category | flops | bytes accessed | tf_op | source)
XLA Modules:
  0.0 72.3 jit_solution(12663774284507304659)
XLA Ops:
  0.7 70.7 %shard_map.73 = f32[512,512]{1,0:T(8,128)S(1)} custom-call(f32[16,512,512]{2,1,0:T(8,128)} %tiles_hbm.1, f32[128,256]{1,0:T(8,128)} %q_hbm.1, f32[256,256]{1,0:T(8,128)} %p_hbm.1, s32[2,16]{1,0:T(2,128)} %bitcast.3, s32[1]{0:T(128)S(6)} %copy.9.counts_hbm, s32[8,16]{1,0:T(8,128)} %bitcast.2, s32[8,16]{1,0:T(8,128)} %col_partner_hbm.1), custom_call_target="tpu_custom_call" | custom-call | tf_op jit(solution)/shard_map/pallas_call | solution.py:467
  71.3 1.0 %copy.10 = f32[512,512]{1,0:T(8,128)} copy(f32[512,512]{1,0:T(8,128)S(1)} %shard_map.73) | data formatting | bytes 2097152
